TPU v7x, 128 devices: a whole 4x4x4 slice. The times are simulated.
128 devices in a mesh: row: 16 (over x, y_hi, core), col: 8 (over z, y_lo).
Axes of the slice: x: 4, y: 4 (y_hi: 2, y_lo: 2; y = y_hi * 2 + y_lo), z: 4, core: 2. Of those that a mesh axis runs over, the one named last changes fastest.
Arguments:
- a_vals: bfloat16 [512, 8, 64, 1024], P('row', 'col'), may hold values from -0.0625 to 0.0625
- a_cols: int32 [512, 8, 16], P('row', 'col'), may hold values from 0 to 63, all different within a row
- p_vals: bfloat16 [512, 64, 256], P(('row', 'col')), may hold values from -1.5 to 1.5
- p_cols: int32 [512, 4], P(('row', 'col')), may hold values from 0 to 15, all different within a row
Outputs:
- coarse_op: float32 [1024, 1024], P('row', 'col')
Inputs may be any that keep to these rules, and one draw needn't show every extreme that they name: `a_cols`: within one fine block row and column range the 16 entries are distinct. `p_cols`: within one fine block row the 4 entries are distinct.
All inputs are finite; a program needn't handle non-finite values.
Results may differ from a plain program's by a relative error of at most 0.0003.
Values may be sent and summed in bfloat16 or wider, within the bound.
No kernel may reach another device: no remote copies, remote signals or barrier semaphores. Data moves between devices by JAX's collectives and lax.ppermute only.
A program may use at most 128 MiB of HBM per device.

v0:
```python
import math
import jax
import jax.numpy as jnp
from jax import lax
from jax.sharding import PartitionSpec as P


def from_root(value, axis, source):
    kept = jnp.where(lax.axis_index(axis) == source, value, 0).astype(value.dtype)
    return lax.psum(kept, axis)


def contract_rows(p_slabs, p_kinds, wide, coarse):
    fine_rows = p_slabs.shape[0]
    block = p_slabs.shape[1]
    touched = p_kinds.shape[1]
    width = wide.shape[1]
    group = math.gcd(fine_rows, 4)
    slabs_g = p_slabs.reshape(fine_rows // group, group, block, touched * block)
    kinds_g = p_kinds.reshape(fine_rows // group, group, touched)
    wide_g = wide.reshape(fine_rows // group, group, block, width)

    def step(total, pieces):
        slab_part, kind_part, wide_part = pieces
        folded = jnp.einsum(
            "ire,irq->ieq",
            slab_part.astype(jnp.float32),
            wide_part,
            precision=lax.Precision.HIGHEST,
        )
        onehot = (kind_part[:, :, None] == lax.iota(jnp.int32, coarse)[None, None, :]).astype(
            jnp.float32
        )
        placed = jnp.einsum(
            "imn,imeq->neq",
            onehot,
            folded.reshape(group, touched, block, width),
            precision=lax.Precision.HIGHEST,
        )
        return (total + placed.reshape(coarse * block, width), None)

    start_total = jnp.zeros((coarse * block, width), jnp.float32)
    total, unused = lax.scan(step, start_total, (slabs_g, kinds_g, wide_g))
    return total


def shards(a_vals, a_cols, p_vals, p_cols):
    n_row = lax.axis_size("row")
    n_col = lax.axis_size("col")
    ratio = n_row // n_col
    block = a_vals.shape[2]
    per_row = a_cols.shape[2]
    touched = p_cols.shape[1]
    fine_rows = a_vals.shape[0]
    col_index = lax.axis_index("col")
    vals_r, ids_r = (
        lax.all_gather(p_vals, "col", axis=0, tiled=True),
        lax.all_gather(p_cols, "col", axis=0, tiled=True),
    )
    got_vals = []
    got_ids = []
    for offset in range(ratio):
        one_vals, one_ids = (
            from_root(vals_r, "row", ratio * col_index + offset),
            from_root(ids_r, "row", ratio * col_index + offset),
        )
        got_vals.append(one_vals)
        got_ids.append(one_ids)
    vals_c = jnp.concatenate(got_vals, axis=0)
    ids_c = jnp.concatenate(got_ids, axis=0)
    group = math.gcd(fine_rows, 4)
    tiles_a = a_vals[:, 0].reshape(fine_rows // group, group, block, per_row, block)
    where_a = a_cols[:, 0].reshape(fine_rows // group, group, per_row)

    def one_group(pair):
        tiles_part, where = pair
        flat_where = where.reshape(-1)
        picked = vals_c[flat_where].reshape(group, per_row, block, touched * block)
        kinds = ids_c[flat_where].reshape(group, per_row * touched)
        product = jnp.einsum(
            "irkf,ikfe->irke", tiles_part, picked, preferred_element_type=jnp.float32
        )
        product = product.reshape(group, block, per_row * touched, block)
        onehot = (kinds[:, :, None] == lax.iota(jnp.int32, n_row)[None, None, :]).astype(
            jnp.float32
        )
        placed = jnp.einsum("irsd,isn->irnd", product, onehot, precision=lax.Precision.HIGHEST)
        return placed.reshape(group * block, n_row * block)

    partial_w = lax.map(one_group, (tiles_a, where_a)).reshape(fine_rows * block, n_row * block)
    rows_out = n_row * block // n_row
    cols_out = n_row * block // n_col
    total = contract_rows(vals_r, ids_r, partial_w, n_row)
    total = total.reshape(n_row, rows_out, n_col, cols_out)
    total = jnp.transpose(total, (0, 2, 1, 3)).reshape(n_row * n_col * rows_out, cols_out)
    return lax.psum_scatter(total, ("row", "col"), scatter_dimension=0, tiled=True)


def solution(mesh):
    in_specs = (
        P("row", "col", None, None),
        P("row", "col", None),
        P(("row", "col"), None, None),
        P(("row", "col"), None),
    )
    out_specs = P("row", "col")
    return jax.shard_map(shards, mesh=mesh, in_specs=in_specs, out_specs=out_specs, check_vma=False)
```

profile of v0, /device:TPU:0, one launch (start us, length us, event | category | flops | bytes accessed | tf_op | source)
XLA Modules:
  0.0 1219.6 jit_solution(4784218886099866676)
XLA Ops:
  7.3 45.0 %all-gather.3.cloned.1.call-done = bf16[32,64,256]{2,1,0:T(8,128)(2,1)} async-done(((bf16[4,64,256]{2,1,0:T(8,128)(2,1)}), bf16[32,64,256]{2,1,0:T(8,128)(2,1)}) %all-gather.3.cloned.1.call-update) | async-done | bytes 1048592 | tf_op jit(solution)/shard_map/all_gather | solution.py:57
  55.1 24.8 %all-gather = s32[8,4,4]{2,1,0:T(4,128)S(1)} all-gather(s32[1,4,4]{2,1,0:T(4,128)S(1)} %bitcast.92), channel_id=1, replica_groups=mesh['row'=16,'col'=8] {'col'}, dimensions={0}, use_global_device_ids=true | all-gather | bytes 576 | tf_op jit(solution)/shard_map/all_gather | solution.py:58
  80.0 13.7 %all-reduce = (s32[32,4]{0,1:T(4,128)S(1)}, s32[32,4]{0,1:T(4,128)S(1)}) all-reduce(s32[32,4]{0,1:T(4,128)S(1)} %copy.32, s32[32,4]{0,1:T(4,128)S(1)} %copy.31), channel_id=1, replica_groups=mesh['row'=16,'col'=8] {'row'}, use_global_device_ids=true, to_apply=%region_3.4 | all-reduce | flops 256 | bytes 2048 | tf_op jit(solution)/shard_map/psum | solution.py:10
  93.9 11.6 reshape_squeeze.7
  105.6 94.5 %all-reduce.4.cloned.1.call-done = (bf16[32,64,256]{2,1,0:T(8,128)(2,1)}, bf16[32,64,256]{2,1,0:T(8,128)(2,1)}) async-done(((bf16[32,64,256]{2,1,0:T(8,128)(2,1)}, bf16[32,64,256]{2,1,0:T(8,128)(2,1)}), (bf16[32,64,256]{2,1,0:T(8,128)(2,1)}, bf16[32,64,256]{2,1,0:T(8,128)(2,1)})) %all-reduce.4.cloned.1.call-update) | async-done | bytes 2097168 | tf_op jit(solution)/shard_map/psum | solution.py:10
  203.2 186.4 %while.21 = (s32[]{:T(128)}, f32[8,256,1024]{2,1,0:T(8,128)}, s32[8,4,16]{2,1,0:T(4,128)S(1)}, s32[64,4]{1,0:T(8,128)S(1)}, bf16[64,64,256]{2,1,0:T(8,128)(2,1)}, /*index=5*/bf16[8,4,64,16,64]{4,3,2,1,0:T(8,128)(2,1)}, s32[]{:T(128)}) while((s32[]{:T(128)}, f32[8,256,1024]{2,1,0:T(8,128)}, s32[8,4,16]{2,1,0:T(4,128)S(1)}, ...), condition=%wide.region_5.6_spmd, body=%wide.region_4.5_spmd.sunk | while | flops 335549632 | bytes 38285140 | solution.py:90
  207.7 4.3 copy.46
  212.0 7.0 reshape.107
  219.7 5.2 convolution_bitcast_fusion.5
  231.0 4.3 copy.46
  235.4 7.0 reshape.107
  243.0 5.2 convolution_bitcast_fusion.5
  254.3 4.3 copy.46
  258.6 7.0 reshape.107
  266.3 5.2 convolution_bitcast_fusion.5
  277.6 4.3 copy.46
  281.9 7.0 reshape.107
  289.6 5.1 convolution_bitcast_fusion.5
  300.9 4.3 copy.46
  305.2 7.0 reshape.107
  312.9 5.2 convolution_bitcast_fusion.5
  324.2 4.3 copy.46
  328.6 7.0 reshape.107
  336.2 5.2 convolution_bitcast_fusion.5
  347.5 4.3 copy.46
  351.8 7.0 reshape.107
  359.5 5.2 convolution_bitcast_fusion.5
  370.8 4.3 copy.46
  375.1 7.0 reshape.107
  382.8 5.2 convolution_bitcast_fusion.5
  389.5 165.1 %while.22 = (s32[]{:T(128)}, f32[1024,1024]{1,0:T(8,128)}, s32[8,4,4]{2,1,0:T(4,128)S(1)}, bf16[8,4,64,256]{3,2,1,0:T(8,128)(2,1)}, f32[8,4,64,1024]{3,2,1,0:T(8,128)}, /*index=5*/s32[]{:T(128)}, s32[]{:T(128)}) while((s32[]{:T(128)}, f32[1024,1024]{1,0:T(8,128)}, s32[8,4,4]{2,1,0:T(4,128)S(1)}, bf16[8,4,64,256]{3,2,1,0:T(8,128)(2,1)}, ...), condition=%wide.region_7.8_spmd.clone, body=%wide.region_6.7_spmd.clone.sunk | while | flops 1008730368 | bytes 34735384 | solution.py:43
  389.6 3.2 fusion.38
  392.7 6.4 fusion.39
  399.1 4.4 copy.48
  403.5 5.6 bitcast_add_fusion.2
  412.3 6.4 fusion.39
  418.6 4.4 copy.48
  423.0 6.9 bitcast_add_fusion.2
  429.9 3.2 fusion.38
  433.1 6.4 fusion.39
  439.4 4.4 copy.48
  443.8 6.9 bitcast_add_fusion.2
  450.7 3.2 fusion.38
  453.9 6.4 fusion.39
  460.2 4.4 copy.48
  464.6 6.9 bitcast_add_fusion.2
  471.5 3.2 fusion.38
  474.7 6.4 fusion.39
  481.0 4.4 copy.48
  485.4 6.9 bitcast_add_fusion.2
  492.3 3.2 fusion.38
  495.5 6.4 fusion.39
  501.8 4.4 copy.48
  506.2 6.9 bitcast_add_fusion.2
  513.1 3.2 fusion.38
  516.3 6.4 fusion.39
  522.6 4.4 copy.48
  527.0 6.9 bitcast_add_fusion.2
  533.9 3.2 fusion.38
  537.1 6.4 fusion.39
  543.4 4.4 copy.48
  547.8 6.9 bitcast_add_fusion.2
  554.7 3.2 copy.34
  560.6 652.5 %reduce-scatter.2.cloned.1.call-done = f32[64,128]{1,0:T(8,128)} async-done(((f32[8192,128]{1,0:T(8,128)}), f32[64,128]{1,0:T(8,128)}) %reduce-scatter.2.cloned.1.call-update) | async-done | bytes 32784 | tf_op jit(solution)/shard_map/reduce_scatter | solution.py:96
  (118 shorter events, 67.3 us)
Async XLA Ops:
  6.5 48.5 %copy-start.1 = (s32[4,4]{1,0:T(4,128)S(1)}, s32[4,4]{1,0:T(4,128)}, u32[]{:S(2)}) copy-start(s32[4,4]{1,0:T(4,128)} %param.11) | copy-start | bytes 196
  6.5 45.8 %all-gather.3.cloned.1.call-start = ((), (), s32[]{:S(2)}) async-start(), calls=%async_computation.1 | async-start | bytes 1179648 | tf_op jit(solution)/shard_map/all_gather | solution.py:57
  7.3 192.9 %all-reduce.4.cloned.1.call-start = ((), (), s32[]{:S(2)}) async-start(), calls=%async_computation.3 | async-start | bytes 4194304 | tf_op jit(solution)/shard_map/psum | solution.py:10
  55.0 1158.1 %reduce-scatter.2.cloned.1.call-start = ((), (), s32[]{:S(2)}) async-start(), calls=%async_computation.2 | async-start | bytes 4227072 | tf_op jit(solution)/shard_map/reduce_scatter | solution.py:96
  93.9 11.6 copy-start
Sparse Core Ops, SparseCore 0:
  9.0 43.3 all-gather.2
  55.1 144.9 all-reduce.3
  560.7 652.3 reduce-scatter.1
where the time goes:
time: 1220 us
  waiting for transfers between devices  793 us (65%)
  local copies, waits for them, and re-layouts  192 us (16%)
  matrix products  123 us (10%)
  other arithmetic  59.6 us (5%)
  blocking collectives  38.5 us (3%)
  between operations  13.2 us (1%)
    reduce_scatter x1, waiting for transfers between devices, shards(): lax.psum_scatter(total, ('row', 'col'), scatter_dimension=0, tiled=True)  653 us
    psum x1, waiting for transfers between devices, from_root(): return lax.psum(kept, axis)  94.5 us
    reshape x8, local copies, waits for them, and re-layouts, one_group(): product = product.reshape(group, block, per_row * touched, block)  55.7 us
    add x8, other arithmetic, step(): return (total + placed.reshape(coarse * block, width), None)  53.6 us
    dot_general x8, matrix products, step(): jnp.einsum('imn,imeq->neq', onehot, folded.reshape(group, touched, block,...  50.8 us
    all_gather x1, waiting for transfers between devices, shards(): lax.all_gather(p_vals, 'col', axis=0, tiled=True)  45 us
    dot_general x8, matrix products, one_group(): jnp.einsum('irsd,isn->irnd', product, onehot, precision=lax.Precision.HIG...  41.2 us
    dot_general x8, local copies, waits for them, and re-layouts, step(): jnp.einsum('imn,imeq->neq', onehot, folded.reshape(group, touched, block,...  35 us
  transfers between devices with their start and end apart: 3, of which 3 were waited for; matrix products, arithmetic and copies ran while one was open for 1% of the time, Pallas kernels for 0%

commit v1 on v0

--- a/solution.py
+++ b/solution.py
@@ -54,7 +54,9 @@
     fine_rows = a_vals.shape[0]
     col_index = lax.axis_index("col")
     vals_r, ids_r = (
-        lax.all_gather(p_vals, "col", axis=0, tiled=True),
+        jnp.concatenate(
+            lax.all_to_all(jnp.stack([p_vals] * lax.axis_size("col")), "col", 0, 0), axis=0
+        ),
         lax.all_gather(p_cols, "col", axis=0, tiled=True),
     )
     got_vals = []

time: 1220 us -> 1200 us (0.984)
  waiting for transfers between devices: 793 us -> 761 us
    all_gather x1 -> x0, waiting for transfers between devices: 45 us -> none  [shards(): lax.all_gather(p_vals, 'col', axis=0, tiled=True)]
    all_to_all x0 -> x1, waiting for transfers between devices: none -> 15.6 us  [shards(): lax.all_to_all(jnp.stack([p_vals] * lax.axis_size('col')), 'col', 0, 0)]
where the time goes in v1:
time: 1200 us
  waiting for transfers between devices  761 us (63%)
  local copies, waits for them, and re-layouts  194 us (16%)
  matrix products  123 us (10%)
  other arithmetic  58.5 us (5%)
  blocking collectives  38.6 us (3%)
  between operations  13.5 us (1%)
    reduce_scatter x1, waiting for transfers between devices, shards(): lax.psum_scatter(total, ('row', 'col'), scatter_dimension=0, tiled=True)  651 us
    psum x1, waiting for transfers between devices, from_root(): return lax.psum(kept, axis)  94.5 us
    reshape x8, local copies, waits for them, and re-layouts, one_group(): product = product.reshape(group, block, per_row * touched, block)  55.7 us
    add x8, other arithmetic, step(): return (total + placed.reshape(coarse * block, width), None)  53.6 us
    dot_general x8, matrix products, step(): jnp.einsum('imn,imeq->neq', onehot, folded.reshape(group, touched, block,...  50.8 us
    dot_general x8, matrix products, one_group(): jnp.einsum('irsd,isn->irnd', product, onehot, precision=lax.Precision.HIG...  41.2 us
    dot_general x8, local copies, waits for them, and re-layouts, step(): jnp.einsum('imn,imeq->neq', onehot, folded.reshape(group, touched, block,...  35 us
    transpose x8, local copies, waits for them, and re-layouts, one_group(): jnp.einsum('irkf,ikfe->irke', tiles_part, picked, preferred_element_type=...  34.8 us
  transfers between devices with their start and end apart: 3, of which 3 were waited for; matrix products, arithmetic and copies ran while one was open for 1% of the time, Pallas kernels for 0%

profile of v1, /device:TPU:0, one launch (start us, length us, event | category | flops | bytes accessed | tf_op | source)
XLA Modules:
  0.0 1195.7 jit_solution(2940824726113619410)
XLA Ops:
  8.5 6.4 all-to-all-start
  15.0 15.6 %all-to-all-done = bf16[8,4,64,256]{3,2,1,0:T(8,128)(2,1)S(1)} async-done(((bf16[8,4,64,256]{3,2,1,0:T(8,128)(2,1)}), bf16[8,4,64,256]{3,2,1,0:T(8,128)(2,1)S(1)}, u32[]{:S(2)}, u32[]{:S(2)}) %all-to-all-start) | async-done | bytes 1048608 | tf_op jit(solution)/shard_map/all_to_all | solution.py:58
  32.3 24.9 %all-gather = s32[8,4,4]{2,1,0:T(4,128)S(1)} all-gather(s32[1,4,4]{2,1,0:T(4,128)S(1)} %bitcast.94), channel_id=1, replica_groups=mesh['row'=16,'col'=8] {'col'}, dimensions={0}, use_global_device_ids=true | all-gather | bytes 576 | tf_op jit(solution)/shard_map/all_gather | solution.py:60
  57.4 13.7 %all-reduce = (s32[32,4]{0,1:T(4,128)S(1)}, s32[32,4]{0,1:T(4,128)S(1)}) all-reduce(s32[32,4]{0,1:T(4,128)S(1)} %copy.32, s32[32,4]{0,1:T(4,128)S(1)} %copy.31), channel_id=1, replica_groups=mesh['row'=16,'col'=8] {'row'}, use_global_device_ids=true, to_apply=%region_3.4 | all-reduce | flops 256 | bytes 2048 | tf_op jit(solution)/shard_map/psum | solution.py:10
  71.2 11.6 reshape_squeeze.7
  83.0 94.5 %all-reduce.4.cloned.1.call-done = (bf16[32,64,256]{2,1,0:T(8,128)(2,1)}, bf16[32,64,256]{2,1,0:T(8,128)(2,1)}) async-done(((bf16[32,64,256]{2,1,0:T(8,128)(2,1)}, bf16[32,64,256]{2,1,0:T(8,128)(2,1)}), (bf16[32,64,256]{2,1,0:T(8,128)(2,1)}, bf16[32,64,256]{2,1,0:T(8,128)(2,1)})) %all-reduce.4.cloned.1.call-update) | async-done | bytes 2097168 | tf_op jit(solution)/shard_map/psum | solution.py:10
  180.5 186.3 %while.21 = (s32[]{:T(128)}, f32[8,256,1024]{2,1,0:T(8,128)}, s32[8,4,16]{2,1,0:T(4,128)S(1)}, s32[64,4]{1,0:T(8,128)S(1)}, bf16[64,64,256]{2,1,0:T(8,128)(2,1)}, /*index=5*/bf16[8,4,64,16,64]{4,3,2,1,0:T(8,128)(2,1)}, s32[]{:T(128)}) while((s32[]{:T(128)}, f32[8,256,1024]{2,1,0:T(8,128)}, s32[8,4,16]{2,1,0:T(4,128)S(1)}, ...), condition=%wide.region_5.6_spmd, body=%wide.region_4.5_spmd.sunk | while | flops 335549632 | bytes 38285140 | solution.py:92
  185.0 4.3 copy.46
  189.4 7.0 reshape.112
  197.0 5.2 convolution_bitcast_fusion.5
  208.4 4.3 copy.46
  212.7 7.0 reshape.112
  220.4 5.1 convolution_bitcast_fusion.5
  231.6 4.3 copy.46
  236.0 7.0 reshape.112
  243.6 5.1 convolution_bitcast_fusion.5
  254.9 4.3 copy.46
  259.2 7.0 reshape.112
  266.9 5.1 convolution_bitcast_fusion.5
  278.2 4.3 copy.46
  282.6 7.0 reshape.112
  290.2 5.2 convolution_bitcast_fusion.5
  301.5 4.3 copy.46
  305.9 7.0 reshape.112
  313.5 5.2 convolution_bitcast_fusion.5
  324.8 4.3 copy.46
  329.2 7.0 reshape.112
  336.8 5.1 convolution_bitcast_fusion.5
  348.1 4.3 copy.46
  352.4 7.0 reshape.112
  360.1 5.2 convolution_bitcast_fusion.5
  366.9 165.1 %while.22 = (s32[]{:T(128)}, f32[1024,1024]{1,0:T(8,128)}, s32[8,4,4]{2,1,0:T(4,128)S(1)}, bf16[8,4,64,256]{3,2,1,0:T(8,128)(2,1)}, f32[8,4,64,1024]{3,2,1,0:T(8,128)}, /*index=5*/s32[]{:T(128)}, s32[]{:T(128)}) while((s32[]{:T(128)}, f32[1024,1024]{1,0:T(8,128)}, s32[8,4,4]{2,1,0:T(4,128)S(1)}, bf16[8,4,64,256]{3,2,1,0:T(8,128)(2,1)}, ...), condition=%wide.region_7.8_spmd.clone, body=%wide.region_6.7_spmd.clone.sunk | while | flops 1008730368 | bytes 34735384 | solution.py:43
  366.9 3.2 fusion.38
  370.1 6.4 fusion.39
  376.4 4.4 copy.48
  380.8 5.6 bitcast_add_fusion.2
  386.4 3.2 fusion.38
  389.6 6.4 fusion.39
  396.0 4.4 copy.48
  400.3 6.9 bitcast_add_fusion.2
  407.2 3.2 fusion.38
  410.4 6.4 fusion.39
  416.8 4.4 copy.48
  421.1 6.9 bitcast_add_fusion.2
  428.0 3.2 fusion.38
  431.2 6.4 fusion.39
  437.6 4.4 copy.48
  441.9 6.9 bitcast_add_fusion.2
  452.0 6.4 fusion.39
  458.4 4.4 copy.48
  462.7 6.9 bitcast_add_fusion.2
  469.6 3.2 fusion.38
  472.8 6.4 fusion.39
  479.2 4.4 copy.48
  483.5 6.9 bitcast_add_fusion.2
  493.6 6.4 fusion.39
  500.0 4.4 copy.48
  504.3 6.9 bitcast_add_fusion.2
  511.2 3.2 fusion.38
  514.4 6.4 fusion.39
  520.8 4.4 copy.48
  525.1 6.9 bitcast_add_fusion.2
  532.0 3.2 copy.34
  537.9 650.9 %reduce-scatter.2.cloned.1.call-done = f32[64,128]{1,0:T(8,128)} async-done(((f32[8192,128]{1,0:T(8,128)}), f32[64,128]{1,0:T(8,128)}) %reduce-scatter.2.cloned.1.call-update) | async-done | bytes 32784 | tf_op jit(solution)/shard_map/reduce_scatter | solution.py:98
  (120 shorter events, 70.7 us)
Async XLA Ops:
  6.5 25.8 %copy-start.2 = (s32[4,4]{1,0:T(4,128)S(1)}, s32[4,4]{1,0:T(4,128)}, u32[]{:S(2)}) copy-start(s32[4,4]{1,0:T(4,128)} %param.11) | copy-start | bytes 196
  8.5 22.1 %all-to-all-start = ((bf16[8,4,64,256]{3,2,1,0:T(8,128)(2,1)}), bf16[8,4,64,256]{3,2,1,0:T(8,128)(2,1)S(1)}, u32[]{:S(2)}, u32[]{:S(2)}) async-start(bf16[8,4,64,256]{3,2,1,0:T(8,128)(2,1)} %stack.2), calls=%async_computation | async-start | bytes 2097152 | tf_op jit(solution)/shard_map/all_to_all | solution.py:58
  15.0 162.5 %all-reduce.4.cloned.1.call-start = ((), (), s32[]{:S(2)}) async-start(), calls=%async_computation.3 | async-start | bytes 4194304 | tf_op jit(solution)/shard_map/psum | solution.py:10
  30.7 52.2 %copy-start = (bf16[8,4,64,256]{3,2,1,0:T(8,128)(2,1)}, bf16[8,4,64,256]{3,2,1,0:T(8,128)(2,1)S(1)}, u32[]{:S(2)}) copy-start(bf16[8,4,64,256]{3,2,1,0:T(8,128)(2,1)S(1)} %all-to-all-done) | copy-start | bytes 3145732
  32.2 1156.6 %reduce-scatter.2.cloned.1.call-start = ((), (), s32[]{:S(2)}) async-start(), calls=%async_computation.2 | async-start | bytes 4227072 | tf_op jit(solution)/shard_map/reduce_scatter | solution.py:98
  71.2 11.6 copy-start.1
Sparse Core Ops, SparseCore 0:
  32.4 145.0 all-reduce.3
  538.0 650.7 reduce-scatter.1
